TPU v7x, 256 devices: a whole 4x4x8 slice. The times are simulated.
256 devices in a mesh: dp: 64 (over z_hi, x, y, core), slab: 4 (over z_lo).
Axes of the slice: x: 4, y: 4, z: 8 (z_hi: 2, z_lo: 4; z = z_hi * 4 + z_lo), core: 2. Of those that a mesh axis runs over, the one named last changes fastest.
Arguments:
- images: bfloat16 [64, 256, 32, 128], P('dp', 'slab'), may hold values from -6 to 6
- cotangent: bfloat16 [64, 128, 64, 256], P('dp', None, 'slab'), may hold values from -6 to 6
- kernel: bfloat16 [3, 3, 256, 128], replicated, may hold values from -0.125 to 0.125
Outputs:
- grad_images: bfloat16 [64, 256, 32, 128], P('dp', 'slab')
- grad_kernel: float32 [3, 3, 256, 128], replicated
All inputs are finite; a program needn't handle non-finite values.
Results may differ from a plain program's by a relative error of at most 0.0034.
Values may be sent and summed in bfloat16 or wider, within the bound.
No kernel may reach another device: no remote copies, remote signals or barrier semaphores. Data moves between devices by JAX's collectives and lax.ppermute only.
A program may use at most 64 MiB of HBM per device.

v0:
```python
import jax
import jax.numpy as jnp
from jax import lax
from jax.sharding import PartitionSpec as P


def extended(cells, sides, width):
    for axis, dim in sides:
        count = lax.axis_size(axis)
        ends = count - 1
        head = lax.slice_in_dim(cells, 0, width, axis=dim)
        tail = lax.slice_in_dim(cells, cells.shape[dim] - width, cells.shape[dim], axis=dim)
        cells = jnp.concatenate(
            [
                lax.ppermute(tail, axis, [(i, (i + 1) % count) for i in range(ends)]),
                cells,
                lax.ppermute(head, axis, [((i + 1) % count, i) for i in range(ends)]),
            ],
            axis=dim,
        )
    return cells


def upsample(field):
    return jnp.repeat(jnp.repeat(field, 2, axis=2), 2, axis=3)


def downsum(field):
    count, chans, rows, cols = field.shape
    return field.reshape(count, chans, rows // 2, 2, cols // 2, 2).sum(axis=(3, 5))


def kernel_terms(padded_up, grad_rows):
    return lax.conv_general_dilated(
        padded_up,
        grad_rows,
        (1, 1),
        ((0, 0), (1, 1)),
        dimension_numbers=("CNHW", "IOHW", "HWNC"),
        preferred_element_type=jnp.float32,
    )


def input_terms(padded_grad, kernel):
    flipped = kernel[::-1, ::-1]
    return lax.conv_general_dilated(
        padded_grad,
        flipped,
        (1, 1),
        ((0, 0), (1, 1)),
        dimension_numbers=("NCHW", "HWOI", "NCHW"),
        preferred_element_type=jnp.float32,
    )


def body(images, cotangent, kernel):
    slab_up = lax.all_to_all(upsample(images), "slab", split_axis=2, concat_axis=1, tiled=True)
    padded_up = extended(slab_up, (("slab", 2),), 1)
    padded_grad = extended(cotangent, (("slab", 2),), 1)
    partial_kernel = kernel_terms(padded_up, cotangent)
    grad_low = downsum(input_terms(padded_grad, kernel))
    returned = lax.all_to_all(
        grad_low.astype(jnp.bfloat16), "slab", split_axis=1, concat_axis=2, tiled=True
    ).astype(grad_low.dtype)
    total = lax.psum(partial_kernel, ("dp", "slab"))
    return (returned.astype(jnp.bfloat16), total)


def solution(mesh):
    placed = (P("dp", "slab", None, None), P("dp", None, "slab", None), P())
    return jax.shard_map(
        body,
        mesh=mesh,
        in_specs=placed,
        out_specs=(P("dp", "slab", None, None), P()),
        check_vma=False,
    )
```

profile of v0, /device:TPU:6, one launch (start us, length us, event | category | flops | bytes accessed | tf_op | source)
XLA Modules:
  0.0 440.7 jit_solution(2120381636830538440)
XLA Ops:
  7.2 0.0 copy-start
  7.2 1.3 copy.36
  8.5 1.3 broadcast_in_dim.10
  9.8 4.7 %copy.37 = bf16[64,64,128]{1,0,2:T(8,128)(2,1)S(1)} copy(bf16[64,64,128]{2,0,1:T(8,128)(2,1)} %bitcast.38) | data formatting | bytes 2097152 | tf_op jit(solution)/shard_map/broadcast_in_dim | solution.py:25
  14.5 3.3 broadcast_in_dim.12
  17.8 7.8 %copy.38 = bf16[1,64,64,256]{3,1,0,2:T(8,128)(2,1)} copy(bf16[1,64,64,256]{2,1,3,0:T(8,128)(2,1)} %bitcast.35) | data formatting | bytes 4194304 | tf_op jit(solution)/shard_map/broadcast_in_dim | solution.py:25
  25.6 5.9 %all-to-all-start.1 = ((bf16[1,64,64,256]{3,1,0,2:T(8,128)(2,1)}), bf16[1,64,64,256]{3,1,0,2:T(8,128)(2,1)S(1)}, u32[]{:S(2)}, u32[]{:S(2)}) async-start(bf16[1,64,64,256]{3,1,0,2:T(8,128)(2,1)} %copy.38), calls=%async_computation.1 | async-start | bytes 4194304 | tf_op jit(solution)/shard_map/all_to_all | solution.py:57
  31.5 1.4 fusion.14
  32.9 3.9 collective-permute-start
  36.8 1.5 collective-permute-start.1
  38.3 4.5 %copy.44 = bf16[1,128,16,256]{1,0,3,2:T(2,128)(2,1)} copy(bf16[1,128,16,256]{3,2,1,0:T(8,128)(2,1)} %param.4) | data formatting | bytes 2097152 | tf_op args[1]
  42.8 25.4 %collective-permute-done = bf16[1,128,1,256]{3,2,1,0:T(2,128)(2,1)S(1)} collective-permute-done((bf16[1,128,1,256]{3,2,1,0:T(2,128)(2,1)S(1)}, bf16[1,128,1,256]{3,2,1,0:T(2,128)(2,1)S(1)}, u32[]{:S(2)}, u32[]{:S(2)}) %collective-permute-start) | collective-permute-done | bytes 65568 | tf_op jit(solution)/shard_map/ppermute | solution.py:15
  68.2 0.0 collective-permute-done.1
  68.2 3.4 maximum_bitcast_fusion
  71.6 2.7 copy.45
  74.3 2.6 pad.clone
  76.9 0.0 copy-start.2
  76.9 3.0 reshape.29
  79.9 1.5 copy.32
  81.5 0.0 copy-done
  81.5 0.0 copy-done.2
  81.5 3.0 broadcast_select_fusion
  84.5 3.3 copy.33
  87.9 0.0 all-to-all-done.1
  87.9 1.2 copy.39
  89.0 0.2 copy.40
  89.2 5.1 %copy.41 = bf16[1,256,16,256]{1,0,3,2:T(2,128)(2,1)} copy(bf16[1,256,16,256]{3,2,1,0:T(8,128)(2,1)S(1)} %bitcast.36) | data formatting | bytes 4194304 | tf_op jit(solution)/shard_map/all_to_all | solution.py:57
  94.3 2.3 fusion.13
  96.6 17.5 %collective-permute-start.2 = (bf16[1,256,1,256]{1,0,3,2:T(2,128)(2,1)}, bf16[1,256,1,256]{1,0,3,2:T(2,128)(2,1)}, u32[]{:S(2)}, u32[]{:S(2)}) collective-permute-start(bf16[1,256,1,256]{1,0,3,2:T(2,128)(2,1)} %get-tuple-element.2), channel_id=1, source_target_pairs={{0,1},{1,2},{2,3},{4,5},{5,6},{6,7},{8,9},{9,10},{10,11},{12,13},{... | collective-permute-start | bytes 393224 | tf_op jit(solution)/shard_map/ppermute | solution.py:15
  114.1 1.5 collective-permute-start.3
  115.6 4.6 %slice_bitcast_fusion = f32[1,256,16,256]{1,2,3,0:T(8,128)} fusion(f32[16,1,264,256]{3,0,2,1:T(8,128)} %bitcast.34), kind=kLoop, calls=%fused_computation.2 | loop fusion | bytes 8388608 | tf_op jit(solution)/shard_map/conv_general_dilated | solution.py:46
  120.2 5.8 %reshape.26 = f32[256,8,2,128,2]{0,2,1,4,3:T(2,128)} reshape(f32[1,256,16,256]{1,2,3,0:T(8,128)} %slice_bitcast_fusion) | data formatting | bytes 8388608 | tf_op jit(solution)/shard_map/reshape | solution.py:30
  126.0 0.0 copy-start.1
  126.0 5.9 %reduce_sum.9 = bf16[256,8,128]{0,1,2:T(8,128)(2,1)S(1)} reduce(f32[256,8,2,128,2]{0,2,1,4,3:T(2,128)} %reshape.26, f32[]{:T(128)} %constant.0.clone.1), dimensions={2,4}, to_apply=%region_0.0 | reduce | flops 786432 | bytes 4718596 | tf_op jit(solution)/shard_map/reduce_sum | solution.py:30
  131.9 1.3 copy.34
  133.2 4.2 all-to-all-start
  137.4 0.0 all-reduce.2.cloned.1.call-start
  137.4 0.0 collective-permute-done.2
  137.4 0.0 collective-permute-done.3
  137.5 0.0 copy-done.1
  137.5 30.8 %fusion = f32[3,3,256,128]{3,2,1,0:T(8,128)} fusion(bf16[1,128,16,256]{1,0,3,2:T(2,128)(2,1)S(1)} %copy-done.1, bf16[1,256,1,256]{1,0,3,2:T(2,128)(2,1)} %collective-permute-done.3, bf16[1,256,16,256]{1,0,3,2:T(2,128)(2,1)} %copy.41, bf16[1,256,1,256]{1,0,3,2:T(2,128)(2,1)} %collective-permute-done.2), kind=kOutput, calls=%fused_computation.1 | convolution fusion | flops 2416705536 | bytes 4587520 | tf_op jit(solution)/shard_map/conv_general_dilated | solution.py:34
  168.2 0.0 all-reduce.2.cloned.1.call-update
  168.3 0.0 all-to-all-done
  168.3 1.9 copy.47
  170.2 261.3 %all-reduce.2.cloned.1.call-done = f32[3,3,256,128]{3,2,1,0:T(8,128)} async-done(((f32[3,3,256,128]{3,2,1,0:T(8,128)}), f32[3,3,256,128]{3,2,1,0:T(8,128)}) %all-reduce.2.cloned.1.call-update) | async-done | bytes 1179664 | tf_op jit(solution)/shard_map/psum | solution.py:65
  431.5 2.4 copy.49
  (1 shorter events, 0.0 us)
Async XLA Ops:
  7.2 74.3 %copy-start = (bf16[3,3,256,128]{3,2,1,0:T(8,128)(2,1)S(1)}, bf16[3,3,256,128]{3,2,1,0:T(8,128)(2,1)}, u32[]{:S(2)}) copy-start(bf16[3,3,256,128]{3,2,1,0:T(8,128)(2,1)} %param.5) | copy-start | bytes 1769476
  25.6 62.3 %all-to-all-start.1 = ((bf16[1,64,64,256]{3,1,0,2:T(8,128)(2,1)}), bf16[1,64,64,256]{3,1,0,2:T(8,128)(2,1)S(1)}, u32[]{:S(2)}, u32[]{:S(2)}) async-start(bf16[1,64,64,256]{3,1,0,2:T(8,128)(2,1)} %copy.38), calls=%async_computation.1 | async-start | bytes 4194304 | tf_op jit(solution)/shard_map/all_to_all | solution.py:57
  32.9 35.3 %collective-permute-start = (bf16[1,128,1,256]{3,2,1,0:T(2,128)(2,1)S(1)}, bf16[1,128,1,256]{3,2,1,0:T(2,128)(2,1)S(1)}, u32[]{:S(2)}, u32[]{:S(2)}) collective-permute-start(bf16[1,128,1,256]{3,2,1,0:T(2,128)(2,1)S(1)} %get-tuple-element.4), channel_id=1, source_target_pairs={{0,1},{1,2},{2,3},{4,5},{5,6},{6,7},{8,9},{9,10},{10,11},{12,13},{... | collective-permute-start | bytes 196616 | tf_op jit(solution)/shard_map/ppermute | solution.py:15
  36.8 31.4 %collective-permute-start.1 = (bf16[1,128,1,256]{3,2,1,0:T(2,128)(2,1)S(1)}, bf16[1,128,1,256]{3,2,1,0:T(2,128)(2,1)S(1)}, u32[]{:S(2)}, u32[]{:S(2)}) collective-permute-start(bf16[1,128,1,256]{3,2,1,0:T(2,128)(2,1)S(1)} %get-tuple-element.5), channel_id=1, source_target_pairs={{1,0},{2,1},{3,2},{5,4},{6,5},{7,6},{9,8},{10,9},{11,10},{13,12},{... | collective-permute-start | bytes 196616 | tf_op jit(solution)/shard_map/ppermute | solution.py:17
  76.9 4.6 %copy-start.2 = (pred[8,33]{0,1:T(8,128)(4,1)S(1)}, pred[8,33]{0,1:T(8,128)(4,1)}, u32[]{:S(2)}) copy-start(pred[8,33]{0,1:T(8,128)(4,1)} %constant.8) | copy-start | bytes 796
  96.6 40.8 %collective-permute-start.2 = (bf16[1,256,1,256]{1,0,3,2:T(2,128)(2,1)}, bf16[1,256,1,256]{1,0,3,2:T(2,128)(2,1)}, u32[]{:S(2)}, u32[]{:S(2)}) collective-permute-start(bf16[1,256,1,256]{1,0,3,2:T(2,128)(2,1)} %get-tuple-element.2), channel_id=1, source_target_pairs={{0,1},{1,2},{2,3},{4,5},{5,6},{6,7},{8,9},{9,10},{10,11},{12,13},{... | collective-permute-start | bytes 393224 | tf_op jit(solution)/shard_map/ppermute | solution.py:15
  114.1 23.4 %collective-permute-start.3 = (bf16[1,256,1,256]{1,0,3,2:T(2,128)(2,1)S(1)}, bf16[1,256,1,256]{1,0,3,2:T(2,128)(2,1)}, u32[]{:S(2)}, u32[]{:S(2)}) collective-permute-start(bf16[1,256,1,256]{1,0,3,2:T(2,128)(2,1)S(1)} %get-tuple-element.3), channel_id=1, source_target_pairs={{1,0},{2,1},{3,2},{5,4},{6,5},{7,6},{9,8},{10,9},{11,10},{13,12},{... | collective-permute-start | bytes 393224 | tf_op jit(solution)/shard_map/ppermute | solution.py:17
  126.0 11.5 %copy-start.1 = (bf16[1,128,16,256]{1,0,3,2:T(2,128)(2,1)S(1)}, bf16[1,128,16,256]{1,0,3,2:T(2,128)(2,1)}, u32[]{:S(2)}) copy-start(bf16[1,128,16,256]{1,0,3,2:T(2,128)(2,1)} %copy.44) | copy-start | bytes 3145732
  133.2 35.0 %all-to-all-start = ((bf16[1,256,8,128]{3,2,0,1:T(8,128)(2,1)}), bf16[1,256,8,128]{3,2,0,1:T(8,128)(2,1)}, u32[]{:S(2)}, u32[]{:S(2)}) async-start(bf16[1,256,8,128]{3,2,0,1:T(8,128)(2,1)} %copy.34), calls=%async_computation | async-start | bytes 1048576 | tf_op jit(solution)/shard_map/all_to_all | solution.py:62
  137.4 294.1 %all-reduce.2.cloned.1.call-start = ((), (), s32[]{:S(2)}) async-start(), calls=%async_computation.2 | async-start | bytes 2359296 | tf_op jit(solution)/shard_map/psum | solution.py:65
Sparse Core Ops, SparseCore 0:
  168.4 263.0 all-reduce.1
where the time goes:
time: 442 us; the launch traced here: 441 us
  waiting for transfers between devices  287 us (65%)
  local copies, waits for them, and re-layouts  62.3 us (14%)
  starting transfers between devices  34.5 us (8%)
  matrix products  33.8 us (8%)
  between operations  14.2 us (3%)
  other arithmetic  9.27 us (2%)
    psum x1, waiting for transfers between devices, body(): total = lax.psum(partial_kernel, ('dp', 'slab'))  261 us
    conv_general_dilated x1, matrix products, kernel_terms(): lax.conv_general_dilated(padded_up, grad_rows, (1, 1), ((0, 0), (1, 1)),...  30.8 us
    ppermute x2, waiting for transfers between devices, extended(): lax.ppermute(tail, axis, [(i, (i + 1) % count) for i in range(ends)])  25.4 us
    ppermute x2, starting transfers between devices, extended(): lax.ppermute(tail, axis, [(i, (i + 1) % count) for i in range(ends)])  21.4 us
    broadcast_in_dim x4, local copies, waits for them, and re-layouts, upsample(): return jnp.repeat(jnp.repeat(field, 2, axis=2), 2, axis=3)  17.1 us
    conv_general_dilated x5, local copies, waits for them, and re-layouts, input_terms(): lax.conv_general_dilated(padded_grad, flipped, (1, 1), ((0, 0), (1, 1)),...  12.5 us
    unnamed x9, local copies, waits for them, and re-layouts  9.55 us
  transfers between devices with their start and end apart: 7, of which 2 were waited for; matrix products, arithmetic and copies ran while one was open for 17% of the time, Pallas kernels for 0%

commit v1 on v0

--- a/solution.py
+++ b/solution.py
@@ -62,7 +62,7 @@
     returned = lax.all_to_all(
         grad_low.astype(jnp.bfloat16), "slab", split_axis=1, concat_axis=2, tiled=True
     ).astype(grad_low.dtype)
-    total = lax.psum(partial_kernel, ("dp", "slab"))
+    total = lax.psum(lax.psum(partial_kernel, axis_name="dp"), axis_name="slab")
     return (returned.astype(jnp.bfloat16), total)
 
 

time: 442 us -> 984 us (2.23)
  waiting for transfers between devices: 287 us -> 797 us
  blocking collectives: 0 us -> 73 us
  starting transfers between devices: 34.5 us -> 8.62 us
  local copies, waits for them, and re-layouts: 62.3 us -> 52.1 us
    psum x1 -> x2, waiting for transfers between devices: 261 us -> 789 us  [body(): total = lax.psum(lax.psum(partial_kernel, axis_name='dp'), axis_name='slab')]
    all_to_all x0 -> x2, blocking collectives: none -> 73 us  [the longest x1 53.9 us: body(): lax.all_to_all(upsample(images), 'slab', split_axis=2, concat_axis=1, til...]
    ppermute x2, waiting for transfers between devices: 25.4 us -> 1.2 us  [extended(): lax.ppermute(tail, axis, [(i, (i + 1) % count) for i in range(ends)])]
    ppermute x2, starting transfers between devices: 21.4 us -> 5.77 us  [extended(): lax.ppermute(tail, axis, [(i, (i + 1) % count) for i in range(ends)])]
    all_to_all x2 -> x0, starting transfers between devices: 10.1 us -> none  [the longest x1 5.89 us: body(): lax.all_to_all(upsample(images), 'slab', split_axis=2, concat_axis=1, til...]
  transfers between devices with their start and end apart: 7 -> 6, of which waited for: 2 -> 5; matrix products, arithmetic and copies ran while one was open for 17% -> 3% of each run, Pallas kernels for 0% -> 0%
where the time goes in v1:
time: 984 us; the launch traced here: 983 us
  waiting for transfers between devices  797 us (81%)
  blocking collectives  73 us (7%)
  local copies, waits for them, and re-layouts  52.1 us (5%)
  matrix products  31.5 us (3%)
  between operations  14.2 us (1%)
    psum x2, waiting for transfers between devices, body(): total = lax.psum(lax.psum(partial_kernel, axis_name='dp'), axis_name='slab')  789 us
    all_to_all x1, blocking collectives, body(): lax.all_to_all(upsample(images), 'slab', split_axis=2, concat_axis=1, til...  53.9 us
    conv_general_dilated x1, matrix products, kernel_terms(): lax.conv_general_dilated(padded_up, grad_rows, (1, 1), ((0, 0), (1, 1)),...  28.5 us
  transfers between devices with their start and end apart: 6, of which 5 were waited for; matrix products, arithmetic and copies ran while one was open for 3% of the time, Pallas kernels for 0%

profile of v1, /device:TPU:6, one launch (start us, length us, event | category | flops | bytes accessed | tf_op | source)
XLA Modules:
  0.0 983.0 jit_solution(1813466868000739039)
XLA Ops:
  7.2 0.0 copy-start
  7.2 0.0 all-reduce.3.cloned.1.call-start
  7.2 1.3 copy.36
  8.5 1.3 broadcast_in_dim.10
  9.8 4.7 copy.37
  14.5 3.3 broadcast_in_dim.12
  17.8 7.0 copy.38
  24.8 53.9 %all_to_all.36 = bf16[1,64,64,256]{3,1,0,2:T(8,128)(2,1)S(1)} all-to-all(bf16[1,64,64,256]{3,1,0,2:T(8,128)(2,1)S(1)} %copy.38), channel_id=1, replica_groups=mesh['dp'=64,'slab'=4] {'slab'}, dimensions={2} | all-to-all | bytes 4194304 | tf_op jit(solution)/shard_map/all_to_all | solution.py:57
  78.7 1.2 copy.39
  79.9 0.2 copy.40
  80.1 5.1 copy.41
  85.2 1.6 fusion.13
  86.7 2.1 collective-permute-start.2
  88.9 1.5 collective-permute-start.3
  90.3 4.5 copy.44
  94.8 0.0 collective-permute-done.2
  94.8 2.3 collective-permute-done.3
  97.1 0.0 copy-start.1
  97.1 28.5 %fusion = f32[3,3,256,128]{3,2,1,0:T(8,128)} fusion(bf16[1,128,16,256]{1,0,3,2:T(2,128)(2,1)} %copy.44, bf16[1,256,1,256]{1,0,3,2:T(2,128)(2,1)S(1)} %collective-permute-done.3, bf16[1,256,16,256]{1,0,3,2:T(2,128)(2,1)} %copy.41, bf16[1,256,1,256]{1,0,3,2:T(2,128)(2,1)S(1)} %collective-permute-done.2), kind=kOutput, calls=%fused_computation.1 | convolution fusion | flops 2416705536 | bytes 4587520 | tf_op jit(solution)/shard_map/conv_general_dilated | solution.py:34
  125.6 0.0 all-reduce.3.cloned.1.call-update
  125.6 0.0 all-reduce.5.cloned.1.call-start
  125.7 0.0 copy-done.1
  125.7 0.2 fusion.14
  125.9 3.6 collective-permute-start
  129.5 1.3 collective-permute-start.1
  130.8 1.2 collective-permute-done
  132.0 4.4 collective-permute-done.1
  136.4 1.1 maximum_bitcast_fusion
  137.5 2.0 copy.45
  139.5 1.6 pad.clone
  141.1 0.0 copy-start.2
  141.1 0.4 reshape.29
  141.6 0.2 copy.32
  141.8 0.0 copy-done
  141.8 0.0 copy-done.2
  141.8 3.0 broadcast_select_fusion
  144.8 3.3 copy.33
  148.1 720.5 %all-reduce.3.cloned.1.call-done = f32[3,3,256,128]{3,2,1,0:T(8,128)} async-done(((f32[3,3,256,128]{3,2,1,0:T(8,128)}), f32[3,3,256,128]{3,2,1,0:T(8,128)}) %all-reduce.3.cloned.1.call-update) | async-done | bytes 1179664 | tf_op jit(solution)/shard_map/psum | solution.py:65
  868.7 0.0 all-reduce.5.cloned.1.call-update
  868.7 4.6 slice_bitcast_fusion
  873.3 5.8 reshape.26
  879.1 5.7 reduce_sum.9
  884.9 0.6 copy.34
  885.4 19.1 %all_to_all.37 = bf16[1,256,8,128]{3,2,0,1:T(8,128)(2,1)S(1)} all-to-all(bf16[1,256,8,128]{3,2,0,1:T(8,128)(2,1)S(1)} %copy.34), channel_id=1, replica_groups=mesh['dp'=64,'slab'=4] {'slab'}, dimensions={1} | all-to-all | bytes 1048576 | tf_op jit(solution)/shard_map/all_to_all | solution.py:62
  904.5 0.9 copy.47
  905.4 68.4 %all-reduce.5.cloned.1.call-done = f32[3,3,256,128]{3,2,1,0:T(8,128)} async-done(((f32[3,3,256,128]{3,2,1,0:T(8,128)}), f32[3,3,256,128]{3,2,1,0:T(8,128)}) %all-reduce.5.cloned.1.call-update) | async-done | bytes 1179664 | tf_op jit(solution)/shard_map/psum | solution.py:65
  973.8 2.4 copy.50
  (1 shorter events, 0.0 us)
Async XLA Ops:
  7.2 134.6 %copy-start = (bf16[3,3,256,128]{3,2,1,0:T(8,128)(2,1)S(1)}, bf16[3,3,256,128]{3,2,1,0:T(8,128)(2,1)}, u32[]{:S(2)}) copy-start(bf16[3,3,256,128]{3,2,1,0:T(8,128)(2,1)} %param.5) | copy-start | bytes 1769476
  7.2 861.5 %all-reduce.3.cloned.1.call-start = ((), (), s32[]{:S(2)}) async-start(), calls=%async_computation.2 | async-start | bytes 2359296 | tf_op jit(solution)/shard_map/psum | solution.py:65
  86.7 8.1 collective-permute-start.2
  88.9 8.3 collective-permute-start.3
  97.1 28.5 %copy-start.1 = (bf16[1,128,16,256]{3,2,1,0:T(8,128)(2,1)S(1)}, bf16[1,128,16,256]{3,2,1,0:T(8,128)(2,1)}, u32[]{:S(2)}) copy-start(bf16[1,128,16,256]{3,2,1,0:T(8,128)(2,1)} %param.4) | copy-start | bytes 3145732
  125.6 848.2 %all-reduce.5.cloned.1.call-start = ((), (), s32[]{:S(2)}) async-start(), calls=%async_computation.3 | async-start | bytes 2359296 | tf_op jit(solution)/shard_map/psum | solution.py:65
  125.9 6.1 collective-permute-start
  129.5 6.9 collective-permute-start.1
  141.1 0.7 copy-start.2
Sparse Core Ops, SparseCore 0:
  125.7 742.8 all-reduce.2
  871.3 102.3 all-reduce.4
